TPU v7x, 32 devices: a whole 2x2x4 slice. The times are simulated.
32 devices in a mesh: row: 4 (over y, core), col: 8 (over z, x).
Axes of the slice: x: 2, y: 2, z: 4, core: 2. Of those that a mesh axis runs over, the one named last changes fastest.
Arguments:
- spectra: float32 [2, 16, 1024, 512], P(None, None, ('col', 'row')), as said below
- pair_mask: int32 [4, 8], P('row', 'col'), may hold values 0 or 1
- band_range: int32 [2], replicated, may hold values from 0 to 512, as said below
Outputs:
- correlations: bfloat16 [1024, 1024, 201], P('row', 'col')
Inputs may be any that keep to these rules, and one draw needn't show every extreme that they name: `spectra`: every channel's spectrum carries its own amplitude. band_range[0] < band_range[1].
All inputs are finite; a program needn't handle non-finite values. No bound on the sum of `pair_mask` on one device may be relied on, other than what follows from the above.
Results may differ from a plain program's by a relative error of at most 0.0061.
Values may be sent and summed in bfloat16 or wider, within the bound.
No kernel may reach another device: no remote copies, remote signals or barrier semaphores. Data moves between devices by JAX's collectives and lax.ppermute only.
A program may use at most 320 MiB of HBM per device.

v0:
```python
import math
import jax
import jax.numpy as jnp
from jax import lax
from jax.sharding import PartitionSpec as P

W = 16
FB = 512
LAGS = 201
NFFT = 15000
F0 = 60
EPS = 1e-06


def whiten(spectra):
    power_mean = jnp.mean(spectra[0] * spectra[0] + spectra[1] * spectra[1], axis=-1, keepdims=True)
    return (spectra * lax.rsqrt(power_mean + EPS)).astype(jnp.bfloat16)


def make_table(band_range):
    freq_index = jnp.arange(FB, dtype=jnp.int32)
    lag_index = jnp.arange(LAGS, dtype=jnp.int32) - LAGS // 2
    turns = jnp.mod((F0 + freq_index)[:, None] * lag_index[None, :], NFFT)
    theta = turns.astype(jnp.float32) * (2.0 * math.pi / NFFT)
    inband = ((freq_index >= band_range[0]) & (freq_index < band_range[1])).astype(jnp.float32)[
        :, None
    ]
    return jnp.concatenate([inband * jnp.cos(theta), -inband * jnp.sin(theta)], axis=0).astype(
        jnp.bfloat16
    )


def pair_block(row_block, col_block, lag_table):
    real_part = jnp.einsum(
        "wap,wbp->abp", row_block[0], col_block[0], preferred_element_type=jnp.float32
    ) + jnp.einsum("wap,wbp->abp", row_block[1], col_block[1], preferred_element_type=jnp.float32)
    imag_part = jnp.einsum(
        "wap,wbp->abp", row_block[1], col_block[0], preferred_element_type=jnp.float32
    ) - jnp.einsum("wap,wbp->abp", row_block[0], col_block[1], preferred_element_type=jnp.float32)
    cross = jnp.stack([real_part, imag_part], axis=2).astype(jnp.bfloat16)
    height = row_block.shape[2]
    width = col_block.shape[2]
    flat = cross.reshape(height * width, 2 * FB)
    summed = jnp.dot(flat, lag_table, preferred_element_type=jnp.float32)
    return (summed * (1.0 / math.sqrt(W * FB))).astype(jnp.bfloat16).reshape(height, width, LAGS)


def body(spectra, pair_mask, band_range):
    whitened = whiten(spectra)
    col_block = lax.all_gather(whitened, "row", axis=2, tiled=True)
    block_width = col_block.shape[2]
    row_count = lax.axis_size("row")
    blocks_per_row = lax.axis_size("col") // row_count
    row_id = lax.axis_index("row")
    col_id = lax.axis_index("col")
    shard_width = whitened.shape[2]
    windows = whitened.shape[1]
    bins = whitened.shape[3]
    strided = lax.all_gather(whitened, "col", axis=2, tiled=True)
    grouped = strided.reshape(2, windows, row_count, blocks_per_row, shard_width, bins)
    moved = lax.all_to_all(grouped, "row", split_axis=2, concat_axis=4, tiled=True)
    row_block = moved.reshape(2, windows, blocks_per_row * row_count * shard_width, bins)
    lag_table = make_table(band_range)
    request = (pair_mask[0, 0] == 1) & (col_id >= row_id * blocks_per_row)
    height = row_block.shape[2]
    return lax.cond(
        request,
        lambda: pair_block(row_block, col_block, lag_table),
        lambda: jnp.zeros((height, block_width, LAGS), jnp.bfloat16),
    )


def solution(mesh):
    return jax.shard_map(
        body,
        mesh=mesh,
        in_specs=(P(None, None, ("col", "row"), None), P("row", "col"), P()),
        out_specs=P("row", "col", None),
        check_vma=False,
    )
```

profile of v0, /device:TPU:0, one launch (start us, length us, event | category | flops | bytes accessed | tf_op | source)
XLA Modules:
  0.0 639.6 jit_solution(6515462427543158156)
XLA Ops:
  6.5 1.7 add_reduce_fusion
  8.3 2.8 multiply_convert_fusion
  11.9 127.0 %all-gather.5.cloned.1.call-done = bf16[2,16,256,512]{3,2,1,0:T(8,128)(2,1)} async-done(((bf16[2,16,32,512]{3,2,1,0:T(8,128)(2,1)}), bf16[2,16,256,512]{3,2,1,0:T(8,128)(2,1)}) %all-gather.5.cloned.1.call-update) | async-done | bytes 8388624 | tf_op jit(solution)/shard_map/all_gather | solution.py:59
  138.9 9.1 %copy.19 = bf16[2,16,4,2,32,512]{5,4,3,1,0,2:T(8,128)(2,1)} copy(bf16[2,16,4,2,32,512]{5,4,3,2,1,0:T(8,128)(2,1)} %bitcast.59) | data formatting | bytes 16777216 | tf_op jit(solution)/shard_map/reshape | solution.py:60
  148.0 5.8 all-to-all-start
  155.0 1.1 fusion.20
  156.1 1.1 fusion.19
  157.3 2.6 multiply_convert_fusion.2
  160.8 27.1 %all-gather.3.cloned.1.call-done = bf16[2,16,128,512]{3,2,1,0:T(8,128)(2,1)} async-done(((bf16[2,16,32,512]{3,2,1,0:T(8,128)(2,1)}), bf16[2,16,128,512]{3,2,1,0:T(8,128)(2,1)}) %all-gather.3.cloned.1.call-update) | async-done | bytes 4194320 | tf_op jit(solution)/shard_map/all_gather | solution.py:50
  187.9 73.7 %all-to-all-done = bf16[2,16,4,2,32,512]{5,4,3,1,0,2:T(8,128)(2,1)} async-done(((bf16[2,16,4,2,32,512]{5,4,3,1,0,2:T(8,128)(2,1)}), bf16[2,16,4,2,32,512]{5,4,3,1,0,2:T(8,128)(2,1)}, u32[]{:S(2)}, u32[]{:S(2)}) %all-to-all-start) | async-done | bytes 8388640 | tf_op jit(solution)/shard_map/all_to_all | solution.py:61
  261.6 371.2 %conditional.1 = (bf16[256,128,201]{1,0,2:T(8,128)(2,1)}) conditional(s32[]{:T(128)} %convert_element_type.30, () %tuple.11, (bf16[2,16,128,512]{3,2,1,0:T(8,128)(2,1)}, bf16[2,16,1,2,4,32,512]{6,5,3,1,0,4,2:T(8,128)(2,1)}, bf16[1024,201]{1,0:T(8,128)(2,1)}) %tuple.12), branch_computations={%region_1.2_spmd, %region_2.3_spmd} | conditional | flops 15750201344 | bytes 807036928 | solution.py:66
  261.6 7.9 %copy.20 = bf16[2,16,128,512]{2,1,3,0:T(8,128)(2,1)} copy(bf16[2,16,128,512]{3,2,1,0:T(8,128)(2,1)} %get-tuple-element.22) | data formatting | bytes 8388608 | tf_op jit(solution)/shard_map
  269.4 6.2 fusion.21
  275.7 7.9 %copy.14 = bf16[16,256,512]{1,0,2:T(8,128)(2,1)} copy(bf16[16,256,512]{2,1,0:T(8,128)(2,1)} %bitcast.57) | data formatting | bytes 8388608 | tf_op jit(solution)/shard_map/cond/branch_1_fun/squeeze | solution.py:35
  283.6 7.8 %copy.15 = bf16[16,256,512]{1,0,2:T(8,128)(2,1)} copy(bf16[16,256,512]{2,1,0:T(8,128)(2,1)} %bitcast.56) | data formatting | bytes 8388608 | tf_op jit(solution)/shard_map/cond/branch_1_fun/squeeze | solution.py:36
  291.4 26.3 %fusion.11 = f32[512,128,256]{2,1,0:T(8,128)} fusion(bf16[16,256,512]{1,0,2:T(8,128)(2,1)} %copy.15, bf16[2,16,128,512]{2,1,3,0:T(8,128)(2,1)} %copy.20), kind=kOutput, calls=%fused_computation.13 | convolution fusion | flops 536870912 | bytes 73400320 | tf_op jit(solution)/shard_map/cond/branch_1_fun/wap,wbp->abp/dot_general | solution.py:37
  317.7 36.4 %fusion.10 = bf16[256,128,1,512]{0,1,3,2:T(8,128)(2,1)} fusion(f32[512,128,256]{2,1,0:T(8,128)} %fusion.11, bf16[16,256,512]{1,0,2:T(8,128)(2,1)} %copy.14, bf16[2,16,128,512]{2,1,3,0:T(8,128)(2,1)} %copy.20), kind=kOutput, calls=%fused_computation.9 | convolution fusion | flops 570425344 | bytes 106954752 | tf_op jit(solution)/shard_map/cond/branch_1_fun/wap,wbp->abp/dot_general | solution.py:39
  354.1 26.3 %fusion.12 = f32[512,128,256]{2,1,0:T(8,128)} fusion(bf16[16,256,512]{1,0,2:T(8,128)(2,1)} %copy.14, bf16[2,16,128,512]{2,1,3,0:T(8,128)(2,1)} %copy.20), kind=kOutput, calls=%fused_computation.14 | convolution fusion | flops 536870912 | bytes 73400320 | tf_op jit(solution)/shard_map/cond/branch_1_fun/wap,wbp->abp/dot_general | solution.py:34
  380.4 36.3 %fusion.9 = bf16[256,128,1,512]{0,1,3,2:T(8,128)(2,1)} fusion(f32[512,128,256]{2,1,0:T(8,128)} %fusion.12, bf16[16,256,512]{1,0,2:T(8,128)(2,1)} %copy.15, bf16[2,16,128,512]{2,1,3,0:T(8,128)(2,1)} %copy.20), kind=kOutput, calls=%fused_computation.8 | convolution fusion | flops 570425344 | bytes 106954752 | tf_op jit(solution)/shard_map/cond/branch_1_fun/wap,wbp->abp/dot_general | solution.py:36
  416.7 44.6 %pad_maximum_fusion = bf16[256,128,2,512]{0,1,3,2:T(8,128)(2,1)} fusion(bf16[256,128,1,512]{0,1,3,2:T(8,128)(2,1)} %fusion.10, bf16[256,128,1,512]{0,1,3,2:T(8,128)(2,1)} %fusion.9), kind=kLoop, calls=%fused_computation.3 | loop fusion | flops 33554432 | bytes 134217728 | tf_op jit(solution)/shard_map/cond/branch_1_fun/stack | solution.py:40
  461.3 81.5 %copy.18 = bf16[256,128,2,512]{1,0,3,2:T(8,128)(2,1)} copy(bf16[256,128,2,512]{0,1,3,2:T(8,128)(2,1)} %pad_maximum_fusion) | data formatting | bytes 134217728 | tf_op jit(solution)/shard_map/cond/branch_1_fun/stack | solution.py:40
  542.8 75.7 %fusion.6 = bf16[32768,201]{0,1:T(8,128)(2,1)} fusion(bf16[1024,201]{1,0:T(8,128)(2,1)S(1)} %copy-done, bf16[128,8,256,128]{3,2,1,0:T(8,128)(2,1)} %bitcast.19), kind=kOutput, calls=%fused_computation.7 | convolution fusion | flops 13502054400 | bytes 80693248 | tf_op jit(solution)/shard_map/cond/branch_1_fun/dot_general | solution.py:44
  618.5 8.4 %copy.23 = bf16[26,8,256,128]{3,2,1,0:T(8,128)(2,1)S(1)} copy(bf16[26,8,256,128]{3,1,2,0:T(8,128)(2,1)} %bitcast.58) | data formatting | bytes 27262976 | tf_op jit(solution)/shard_map/cond
  626.8 6.0 slice_bitcast_fusion
  (13 shorter events, 2.2 us)
Async XLA Ops:
  6.5 132.4 %all-gather.5.cloned.1.call-start = ((), (), s32[]{:S(2)}) async-start(), calls=%async_computation.2 | async-start | bytes 9437184 | tf_op jit(solution)/shard_map/all_gather | solution.py:59
  11.2 176.7 %all-gather.3.cloned.1.call-start = ((), (), s32[]{:S(2)}) async-start(), calls=%async_computation.1 | async-start | bytes 5242880 | tf_op jit(solution)/shard_map/all_gather | solution.py:50
  148.0 6.4 %copy-start.1 = (s32[2]{0:T(128)S(1)}, s32[2]{0:T(128)}, u32[]{:S(2)}) copy-start(s32[2]{0:T(128)} %param.7) | copy-start | bytes 28
  148.0 113.6 %all-to-all-start = ((bf16[2,16,4,2,32,512]{5,4,3,1,0,2:T(8,128)(2,1)}), bf16[2,16,4,2,32,512]{5,4,3,1,0,2:T(8,128)(2,1)}, u32[]{:S(2)}, u32[]{:S(2)}) async-start(bf16[2,16,4,2,32,512]{5,4,3,1,0,2:T(8,128)(2,1)} %copy.19), calls=%async_computation | async-start | bytes 16777216 | tf_op jit(solution)/shard_map/all_to_all | solution.py:61
  461.3 81.5 %copy-start = (bf16[1024,201]{1,0:T(8,128)(2,1)S(1)}, bf16[1024,201]{1,0:T(8,128)(2,1)}, u32[]{:S(2)}) copy-start(bf16[1024,201]{1,0:T(8,128)(2,1)} %get-tuple-element.17) | copy-start | bytes 1234948 | tf_op jit(solution)/shard_map/cond
Sparse Core Ops, SparseCore 0:
  11.3 127.5 all-gather.4
  140.5 47.3 all-gather.2
where the time goes:
time: 643 us; the launch traced here: 640 us
  waiting for transfers between devices  229 us (36%)
  matrix products  201 us (31%)
  local copies, waits for them, and re-layouts  135 us (21%)
  other arithmetic  55 us (9%)
  between operations  14.1 us (2%)
    all_gather x1, waiting for transfers between devices, body(): strided = lax.all_gather(whitened, 'col', axis=2, tiled=True)  127 us
    another operation x1, local copies, waits for them, and re-layouts, pair_block(): cross = jnp.stack([real_part, imag_part], axis=2).astype(jnp.bfloat16)  81.5 us
    dot_general x1, matrix products, pair_block(): summed = jnp.dot(flat, lag_table, preferred_element_type=jnp.float32)  75.7 us
    all_to_all x1, waiting for transfers between devices, body(): lax.all_to_all(grouped, 'row', split_axis=2, concat_axis=4, tiled=True)  73.7 us
    another operation x1, other arithmetic, pair_block(): cross = jnp.stack([real_part, imag_part], axis=2).astype(jnp.bfloat16)  44.6 us
    dot_general x1, matrix products, pair_block(): jnp.einsum('wap,wbp->abp', row_block[0], col_block[1], preferred_element_...  36.4 us
    dot_general x1, matrix products, pair_block(): jnp.einsum('wap,wbp->abp', row_block[1], col_block[1], preferred_element_...  36.3 us
    all_gather x1, waiting for transfers between devices, body(): col_block = lax.all_gather(whitened, 'row', axis=2, tiled=True)  27.1 us
  transfers between devices with their start and end apart: 3, of which 3 were waited for; matrix products, arithmetic and copies ran while one was open for 2% of the time, Pallas kernels for 0%

commit v1 on v0

--- a/solution.py
+++ b/solution.py
@@ -10,6 +10,17 @@
 NFFT = 15000
 F0 = 60
 EPS = 1e-06
+
+
+def turned_line(array, mesh_axis, dim):
+    devices = lax.axis_size(mesh_axis)
+    right = [(i, (i + 1) % devices) for i in range(devices)]
+    terms = [array]
+    for reach in range(1, devices):
+        terms = [lax.ppermute(terms[0], mesh_axis, right), *terms]
+    whole = jnp.concatenate(terms, axis=dim)
+    shift = (lax.axis_index(mesh_axis) + 1) * terms[-1].shape[dim]
+    return jnp.roll(whole, shift, axis=dim)
 
 
 def whiten(spectra):
@@ -47,7 +58,7 @@
 
 def body(spectra, pair_mask, band_range):
     whitened = whiten(spectra)
-    col_block = lax.all_gather(whitened, "row", axis=2, tiled=True)
+    col_block = turned_line(whitened, "row", 2)
     block_width = col_block.shape[2]
     row_count = lax.axis_size("row")
     blocks_per_row = lax.axis_size("col") // row_count

time: 643 us -> 695 us (1.081)
  waiting for transfers between devices: 229 us -> 253 us
  local copies, waits for them, and re-layouts: 135 us -> 155 us
    ppermute x0 -> x3, waiting for transfers between devices: none -> 125 us  [turned_line(): terms = [lax.ppermute(terms[0], mesh_axis, right), *terms]]
    all_to_all x1, waiting for transfers between devices: 73.7 us -> 0.01 us  [body(): lax.all_to_all(grouped, 'row', split_axis=2, concat_axis=4, tiled=True)]
    all_gather x1 -> x0, waiting for transfers between devices: 27.1 us -> none  [body(): col_block = lax.all_gather(whitened, 'row', axis=2, tiled=True)]
    unnamed x2 -> x16, local copies, waits for them, and re-layouts: 0.01 us -> 13.8 us
  transfers between devices with their start and end apart: 3 -> 5, of which waited for: 3 -> 4; matrix products, arithmetic and copies ran while one was open for 2% -> 3% of each run, Pallas kernels for 0% -> 0%
where the time goes in v1:
time: 695 us; the launch traced here: 692 us
  waiting for transfers between devices  253 us (36%)
  matrix products  206 us (30%)
  local copies, waits for them, and re-layouts  155 us (22%)
  other arithmetic  57.8 us (8%)
  between operations  14.1 us (2%)
    all_gather x1, waiting for transfers between devices, body(): strided = lax.all_gather(whitened, 'col', axis=2, tiled=True)  128 us
    ppermute x3, waiting for transfers between devices, turned_line(): terms = [lax.ppermute(terms[0], mesh_axis, right), *terms]  125 us
    another operation x1, local copies, waits for them, and re-layouts, pair_block(): cross = jnp.stack([real_part, imag_part], axis=2).astype(jnp.bfloat16)  81.4 us
    dot_general x1, matrix products, pair_block(): summed = jnp.dot(flat, lag_table, preferred_element_type=jnp.float32)  75.6 us
    another operation x1, other arithmetic, pair_block(): cross = jnp.stack([real_part, imag_part], axis=2).astype(jnp.bfloat16)  44.7 us
    dot_general x1, matrix products, pair_block(): jnp.einsum('wap,wbp->abp', row_block[0], col_block[1], preferred_element_...  37.7 us
    dot_general x1, matrix products, pair_block(): jnp.einsum('wap,wbp->abp', row_block[1], col_block[1], preferred_element_...  37.7 us
    dot_general x1, matrix products, pair_block(): jnp.einsum('wap,wbp->abp', row_block[0], col_block[0], preferred_element_...  27.3 us
  transfers between devices with their start and end apart: 5, of which 4 were waited for; matrix products, arithmetic and copies ran while one was open for 3% of the time, Pallas kernels for 0%

profile of v1, /device:TPU:0, one launch (start us, length us, event | category | flops | bytes accessed | tf_op | source)
XLA Modules:
  0.0 692.1 jit_solution(13538995196087253988)
XLA Ops:
  8.3 2.8 multiply_convert_fusion
  11.2 127.8 %all-gather.2.cloned.1.call-done = bf16[2,16,256,512]{3,2,1,0:T(8,128)(2,1)} async-done(((bf16[2,16,32,512]{3,2,1,0:T(8,128)(2,1)}), bf16[2,16,256,512]{3,2,1,0:T(8,128)(2,1)}) %all-gather.2.cloned.1.call-update) | async-done | bytes 8388624 | tf_op jit(solution)/shard_map/all_gather | solution.py:70
  138.9 8.4 %copy.20 = bf16[2,16,4,2,32,512]{5,4,3,1,0,2:T(8,128)(2,1)} copy(bf16[2,16,4,2,32,512]{5,4,3,2,1,0:T(8,128)(2,1)} %bitcast.59) | data formatting | bytes 16777216 | tf_op jit(solution)/shard_map/reshape | solution.py:71
  147.4 5.9 all-to-all-start
  153.8 103.8 %collective-permute-done = bf16[2,16,32,512]{3,2,1,0:T(8,128)(2,1)S(1)} collective-permute-done((bf16[2,16,32,512]{3,2,1,0:T(8,128)(2,1)S(1)}, bf16[2,16,32,512]{3,2,1,0:T(8,128)(2,1)S(1)}, u32[]{:S(2)}, u32[]{:S(2)}) %collective-permute-start) | collective-permute-done | bytes 1048608 | tf_op jit(solution)/shard_map/ppermute | solution.py:20
  258.6 14.3 %collective-permute-done.1 = bf16[2,16,32,512]{3,2,1,0:T(8,128)(2,1)} collective-permute-done((bf16[2,16,32,512]{3,2,1,0:T(8,128)(2,1)S(1)}, bf16[2,16,32,512]{3,2,1,0:T(8,128)(2,1)}, u32[]{:S(2)}, u32[]{:S(2)}) %collective-permute-start.1) | collective-permute-done | bytes 1048608 | tf_op jit(solution)/shard_map/ppermute | solution.py:20
  276.9 2.6 multiply_convert_fusion.2
  280.4 7.1 %collective-permute-done.2 = bf16[2,16,32,512]{3,2,1,0:T(8,128)(2,1)} collective-permute-done((bf16[2,16,32,512]{3,2,1,0:T(8,128)(2,1)}, bf16[2,16,32,512]{3,2,1,0:T(8,128)(2,1)}, u32[]{:S(2)}, u32[]{:S(2)}) %collective-permute-start.2) | collective-permute-done | bytes 1048608 | tf_op jit(solution)/shard_map/ppermute | solution.py:20
  287.4 2.4 constant_dynamic-update-slice_fusion.7
  292.2 2.4 constant_dynamic-update-slice_fusion.5
  302.8 382.5 %conditional.1 = (bf16[256,128,201]{1,0,2:T(8,128)(2,1)}) conditional(s32[]{:T(128)} %convert_element_type.36, () %tuple.22, (s32[]{:T(128)}, s32[]{:T(128)}, bf16[2,16,256,512]{3,2,1,0:T(8,128)(2,1)}, bf16[2,16,1,2,4,32,512]{6,5,3,1,0,4,2:T(8,128)(2,1)}, bf16[1024,201]{1,0:T(8,128)(2,1)}, /*index=5*/s32[]{:T(128)}, s32[]{:T(128)}) %tuple.29), branch_computations={%region_1.2_spmd, %region_2.3_spmd.clone} | conditional | flops 15750201344 | bytes 815425728 | solution.py:77
  302.8 14.5 %copy.21 = bf16[2,16,256,512]{2,1,3,0:T(8,128)(2,1)} copy(bf16[2,16,256,512]{3,2,1,0:T(8,128)(2,1)} %get-tuple-element.129) | data formatting | bytes 16777216 | tf_op jit(solution)/shard_map
  317.3 6.1 fusion.25
  323.3 7.9 %copy.15 = bf16[16,256,512]{1,0,2:T(8,128)(2,1)} copy(bf16[16,256,512]{2,1,0:T(8,128)(2,1)} %bitcast.57) | data formatting | bytes 8388608 | tf_op jit(solution)/shard_map/cond/branch_1_fun/squeeze | solution.py:46
  331.3 7.9 %copy.16 = bf16[16,256,512]{1,0,2:T(8,128)(2,1)} copy(bf16[16,256,512]{2,1,0:T(8,128)(2,1)} %bitcast.56) | data formatting | bytes 8388608 | tf_op jit(solution)/shard_map/cond/branch_1_fun/squeeze | solution.py:47
  339.2 27.3 %fusion.11 = f32[512,128,256]{2,1,0:T(8,128)} fusion(bf16[16,256,512]{1,0,2:T(8,128)(2,1)} %copy.16, bf16[2,16,256,512]{2,1,3,0:T(8,128)(2,1)} %copy.21, s32[]{:T(128)S(6)} %select_n.30), kind=kOutput, calls=%fused_computation.13 | convolution fusion | flops 536870912 | bytes 73400320 | tf_op jit(solution)/shard_map/cond/branch_1_fun/wap,wbp->abp/dot_general | solution.py:48
  366.5 37.7 %fusion.10 = bf16[256,128,1,512]{0,1,3,2:T(8,128)(2,1)} fusion(f32[512,128,256]{2,1,0:T(8,128)} %fusion.11, bf16[16,256,512]{1,0,2:T(8,128)(2,1)} %copy.15, bf16[2,16,256,512]{2,1,3,0:T(8,128)(2,1)} %copy.21, s32[]{:T(128)S(6)} %add.77, s32[]{:T(128)S(6)} %select_n.30), kind=kOutput, calls=%fused_computation.9 | convolution fusion | flops 570425344 | bytes 106954760 | tf_op jit(solution)/shard_map/cond/branch_1_fun/wap,wbp->abp/dot_general | solution.py:50
  404.2 27.3 %fusion.12 = f32[512,128,256]{2,1,0:T(8,128)} fusion(bf16[16,256,512]{1,0,2:T(8,128)(2,1)} %copy.15, bf16[2,16,256,512]{2,1,3,0:T(8,128)(2,1)} %copy.21, s32[]{:T(128)S(6)} %select_n.30), kind=kOutput, calls=%fused_computation.14 | convolution fusion | flops 536870912 | bytes 73400320 | tf_op jit(solution)/shard_map/cond/branch_1_fun/wap,wbp->abp/dot_general | solution.py:45
  431.5 37.7 %fusion.9 = bf16[256,128,1,512]{0,1,3,2:T(8,128)(2,1)} fusion(f32[512,128,256]{2,1,0:T(8,128)} %fusion.12, bf16[16,256,512]{1,0,2:T(8,128)(2,1)} %copy.16, bf16[2,16,256,512]{2,1,3,0:T(8,128)(2,1)} %copy.21, s32[]{:T(128)S(6)} %add.77, s32[]{:T(128)S(6)} %select_n.30), kind=kOutput, calls=%fused_computation.8 | convolution fusion | flops 570425344 | bytes 106954760 | tf_op jit(solution)/shard_map/cond/branch_1_fun/wap,wbp->abp/dot_general | solution.py:47
  469.2 44.7 %pad_maximum_fusion = bf16[256,128,2,512]{0,1,3,2:T(8,128)(2,1)} fusion(bf16[256,128,1,512]{0,1,3,2:T(8,128)(2,1)} %fusion.10, bf16[256,128,1,512]{0,1,3,2:T(8,128)(2,1)} %fusion.9), kind=kLoop, calls=%fused_computation.3 | loop fusion | flops 33554432 | bytes 134217728 | tf_op jit(solution)/shard_map/cond/branch_1_fun/stack | solution.py:51
  513.9 81.4 %copy.19 = bf16[256,128,2,512]{1,0,3,2:T(8,128)(2,1)} copy(bf16[256,128,2,512]{0,1,3,2:T(8,128)(2,1)} %pad_maximum_fusion) | data formatting | bytes 134217728 | tf_op jit(solution)/shard_map/cond/branch_1_fun/stack | solution.py:51
  595.3 75.6 %fusion.6 = bf16[32768,201]{0,1:T(8,128)(2,1)} fusion(bf16[1024,201]{1,0:T(8,128)(2,1)S(1)} %copy-done.4, bf16[128,8,256,128]{3,2,1,0:T(8,128)(2,1)} %bitcast.19), kind=kOutput, calls=%fused_computation.7 | convolution fusion | flops 13502054400 | bytes 80693248 | tf_op jit(solution)/shard_map/cond/branch_1_fun/dot_general | solution.py:55
  670.9 8.4 %copy.24 = bf16[26,8,256,128]{3,2,1,0:T(8,128)(2,1)S(1)} copy(bf16[26,8,256,128]{3,1,2,0:T(8,128)(2,1)} %bitcast.58) | data formatting | bytes 27262976 | tf_op jit(solution)/shard_map/cond
  679.3 6.0 slice_bitcast_fusion
  (32 shorter events, 17.9 us)
Async XLA Ops:
  6.5 132.4 %all-gather.2.cloned.1.call-start = ((), (), s32[]{:S(2)}) async-start(), calls=%async_computation.1 | async-start | bytes 9437184 | tf_op jit(solution)/shard_map/all_gather | solution.py:70
  147.4 5.9 copy-start.1
  147.4 126.2 %copy-start.5 = (s32[2]{0:T(128)S(1)}, s32[2]{0:T(128)}, u32[]{:S(2)}) copy-start(s32[2]{0:T(128)} %param.7) | copy-start | bytes 28
  147.4 147.2 %copy-start = (f32[2,16,32,512]{3,2,1,0:T(8,128)S(1)}, f32[2,16,32,512]{3,2,1,0:T(8,128)}, u32[]{:S(2)}) copy-start(f32[2,16,32,512]{3,2,1,0:T(8,128)} %param.5) | copy-start | bytes 6291460
  147.4 155.4 %all-to-all-start = ((bf16[2,16,4,2,32,512]{5,4,3,1,0,2:T(8,128)(2,1)}), bf16[2,16,4,2,32,512]{5,4,3,1,0,2:T(8,128)(2,1)}, u32[]{:S(2)}, u32[]{:S(2)}) async-start(bf16[2,16,4,2,32,512]{5,4,3,1,0,2:T(8,128)(2,1)} %copy.20), calls=%async_computation | async-start | bytes 16777216 | tf_op jit(solution)/shard_map/all_to_all | solution.py:72
  153.3 104.3 %collective-permute-start = (bf16[2,16,32,512]{3,2,1,0:T(8,128)(2,1)S(1)}, bf16[2,16,32,512]{3,2,1,0:T(8,128)(2,1)S(1)}, u32[]{:S(2)}, u32[]{:S(2)}) collective-permute-start(bf16[2,16,32,512]{3,2,1,0:T(8,128)(2,1)S(1)} %copy-done.1), channel_id=1, source_target_pairs={{0,8},{8,16},{16,24},{24,0},{1,9},{9,17},{17,25},{25,1},{2,10},{10... | collective-permute-start | bytes 3145736 | tf_op jit(solution)/shard_map/ppermute | solution.py:20
  257.6 1.0 copy-start.2
  258.6 14.3 %collective-permute-start.1 = (bf16[2,16,32,512]{3,2,1,0:T(8,128)(2,1)S(1)}, bf16[2,16,32,512]{3,2,1,0:T(8,128)(2,1)}, u32[]{:S(2)}, u32[]{:S(2)}) collective-permute-start(bf16[2,16,32,512]{3,2,1,0:T(8,128)(2,1)S(1)} %collective-permute-done), channel_id=1, source_target_pairs={{0,8},{8,16},{16,24},{24,0},{1,9},{9,17},{17,25},{25,1},{2,10},{10... | collective-permute-start | bytes 3145736 | tf_op jit(solution)/shard_map/ppermute | solution.py:20
  258.6 41.9 %copy-start.3 = (bf16[2,16,32,512]{3,2,1,0:T(8,128)(2,1)S(1)}, bf16[2,16,32,512]{3,2,1,0:T(8,128)(2,1)}, u32[]{:S(2)}) copy-start(bf16[2,16,32,512]{3,2,1,0:T(8,128)(2,1)} %copy-done.2) | copy-start | bytes 3145732
  272.9 14.5 %collective-permute-start.2 = (bf16[2,16,32,512]{3,2,1,0:T(8,128)(2,1)}, bf16[2,16,32,512]{3,2,1,0:T(8,128)(2,1)}, u32[]{:S(2)}, u32[]{:S(2)}) collective-permute-start(bf16[2,16,32,512]{3,2,1,0:T(8,128)(2,1)} %collective-permute-done.1), channel_id=1, source_target_pairs={{0,8},{8,16},{16,24},{24,0},{1,9},{9,17},{17,25},{25,1},{2,10},{10... | collective-permute-start | bytes 3145736 | tf_op jit(solution)/shard_map/ppermute | solution.py:20
  513.9 81.4 %copy-start.4 = (bf16[1024,201]{1,0:T(8,128)(2,1)S(1)}, bf16[1024,201]{1,0:T(8,128)(2,1)}, u32[]{:S(2)}) copy-start(bf16[1024,201]{1,0:T(8,128)(2,1)} %get-tuple-element.109) | copy-start | bytes 1234948 | tf_op jit(solution)/shard_map/cond
Sparse Core Ops, SparseCore 0:
  11.3 127.5 all-gather.1
